TPU v7x, 256 devices: a whole 4x4x8 slice. The times are simulated.
256 devices in a mesh: inner: 32 (over z, y_hi, core), outer: 8 (over y_lo, x).
Axes of the slice: x: 4, y: 4 (y_hi: 2, y_lo: 2; y = y_hi * 2 + y_lo), z: 8, core: 2. Of those that a mesh axis runs over, the one named last changes fastest.
Arguments:
- queries: bfloat16 [32768, 1024], P(('outer', 'inner')), may hold values from -8 to 8
- key_rows: bfloat16 [32768, 128], P(('outer', 'inner')), may hold values from -8 to 8
- value_rows: bfloat16 [32768, 128], P(('outer', 'inner')), may hold values from -6 to 6
- grad_output: bfloat16 [32768, 1024], P(('outer', 'inner')), may hold values from -6 to 6
- doc_blocks: int32 [256], replicated, may hold values from 0 to 31, never falling along the last dimension, each value on 1 to 32 neighbouring positions
Outputs:
- grad_queries: bfloat16 [32768, 1024], P(('outer', 'inner'))
- grad_keys: bfloat16 [32768, 128], P(('outer', 'inner'))
- grad_values: bfloat16 [32768, 128], P(('outer', 'inner'))
All inputs are finite; a program needn't handle non-finite values.
Results may differ from a plain program's by a relative error of at most 0.019.
Values may be sent and summed in bfloat16 or wider, within the bound.
A program may use at most 64 MiB of HBM per device.

v0:
```python
import jax
import jax.numpy as jnp
from jax import lax
from jax.sharding import PartitionSpec as P


def shifted(block, axis, distance):
    devices = range(lax.axis_size(axis))
    route = [(i - distance, i) for i in devices if i - distance in devices]
    return lax.ppermute(block, axis, route)


def shards(queries, key_rows, value_rows, grad_output, doc_blocks):
    token_count = queries.shape[0]
    width = key_rows.shape[1]
    head_count = queries.shape[1] // width
    inner_count = lax.axis_size("inner")
    outer_count = lax.axis_size("outer")
    inner_at = lax.axis_index("inner")
    outer_at = lax.axis_index("outer")
    blocks_dev = doc_blocks.shape[0] // (inner_count * outer_count)
    block_len = token_count // blocks_dev
    tile_blocks = 4
    span_blocks = inner_count * blocks_dev
    win_blocks = -(-(span_blocks + blocks_dev) // tile_blocks) * tile_blocks
    pad_blocks = max(0, (inner_count - 1) * blocks_dev + win_blocks - 2 * span_blocks)
    tile_count = win_blocks // tile_blocks
    tile_len = tile_blocks * block_len
    scaling = width ** (-0.5)
    earlier_k, earlier_v = shifted((key_rows, value_rows), "outer", 1)
    group_k, group_v, prior_k, prior_v = (
        lax.all_gather(key_rows, "inner", axis=0, tiled=True),
        lax.all_gather(value_rows, "inner", axis=0, tiled=True),
        lax.all_gather(earlier_k, "inner", axis=0, tiled=True),
        lax.all_gather(earlier_v, "inner", axis=0, tiled=True),
    )
    padding = jnp.zeros((pad_blocks * block_len, width), key_rows.dtype)
    keys_all = jnp.concatenate([prior_k, group_k, padding], axis=0)
    values_all = jnp.concatenate([prior_v, group_v, padding], axis=0)
    first_block = inner_at * blocks_dev
    key_win = lax.dynamic_slice_in_dim(keys_all, first_block * block_len, win_blocks * block_len, 0)
    value_win = lax.dynamic_slice_in_dim(
        values_all, first_block * block_len, win_blocks * block_len, 0
    )
    tags_pad = jnp.concatenate(
        [
            jnp.full((span_blocks,), -1, jnp.int32),
            doc_blocks,
            jnp.full((span_blocks + pad_blocks,), -1, jnp.int32),
        ]
    )
    key_tags = lax.dynamic_slice_in_dim(
        tags_pad, outer_at * span_blocks + first_block, win_blocks, 0
    )
    own_tags = lax.dynamic_slice_in_dim(
        doc_blocks, (outer_at * inner_count + inner_at) * blocks_dev, blocks_dev, 0
    )
    row_tags = jnp.repeat(jnp.repeat(own_tags, block_len), head_count)
    row_pos = (
        jnp.repeat(jnp.arange(token_count, dtype=jnp.int32), head_count) + span_blocks * block_len
    )
    key_tiles = key_win.reshape(tile_count, tile_len, width)
    value_tiles = value_win.reshape(tile_count, tile_len, width)
    tag_tiles = jnp.repeat(key_tags, block_len).reshape(tile_count, tile_len)
    pos_tiles = jnp.arange(win_blocks * block_len, dtype=jnp.int32).reshape(tile_count, tile_len)
    query_flat = queries.reshape(token_count * head_count, width)
    grad_flat = grad_output.reshape(token_count * head_count, width)
    row_total = token_count * head_count

    def allowed_of(tag_tile, pos_tile):
        return (row_tags[:, None] == tag_tile[None, :]) & (pos_tile[None, :] <= row_pos[:, None])

    def forward_tile(running, pieces):
        key_tile, value_tile, tag_tile, pos_tile = pieces
        allowed = allowed_of(tag_tile, pos_tile)
        row_max, row_sum, out_acc = running
        scores = (
            jnp.einsum("rd,kd->rk", query_flat, key_tile, preferred_element_type=jnp.float32)
            * scaling
        )
        masked = jnp.where(allowed, scores, -jnp.inf)
        new_max = jnp.maximum(row_max, jnp.max(masked, axis=1, keepdims=True))
        factor = jnp.exp(row_max - new_max)
        weights = jnp.exp(masked - new_max)
        new_sum = row_sum * factor + jnp.sum(weights, axis=1, keepdims=True)
        weights_high = weights.astype(jnp.bfloat16)
        weights_rest = (weights - weights_high.astype(jnp.float32)).astype(jnp.bfloat16)
        product = jnp.dot(weights_high, value_tile, preferred_element_type=jnp.float32)
        product = product + jnp.dot(weights_rest, value_tile, preferred_element_type=jnp.float32)
        new_out = out_acc * factor + product
        return ((new_max, new_sum, new_out), None)

    start_state = (
        jnp.full((row_total, 1), -1e30, jnp.float32),
        jnp.zeros((row_total, 1), jnp.float32),
        jnp.zeros((row_total, width), jnp.float32),
    )
    (row_max, row_sum, out_acc), unused_ys = lax.scan(
        forward_tile, start_state, (key_tiles, value_tiles, tag_tiles, pos_tiles)
    )
    attn_out = out_acc / row_sum
    delta = jnp.sum(grad_flat.astype(jnp.float32) * attn_out, axis=1, keepdims=True)

    def backward_tile(grad_q, pieces):
        key_tile, value_tile, tag_tile, pos_tile = pieces
        allowed = allowed_of(tag_tile, pos_tile)
        scores = (
            jnp.einsum("rd,kd->rk", query_flat, key_tile, preferred_element_type=jnp.float32)
            * scaling
        )
        probs = jnp.exp(jnp.where(allowed, scores - row_max, -jnp.inf)) / row_sum
        probs_low = probs.astype(jnp.bfloat16)
        value_part = jnp.einsum(
            "rk,rd->kd", probs_low, grad_flat, preferred_element_type=jnp.float32
        )
        dprobs = jnp.einsum("rd,kd->rk", grad_flat, value_tile, preferred_element_type=jnp.float32)
        dscores = (probs * (dprobs - delta) * scaling).astype(jnp.bfloat16)
        new_q = grad_q + jnp.dot(dscores, key_tile, preferred_element_type=jnp.float32)
        key_part = jnp.einsum("rk,rd->kd", dscores, query_flat, preferred_element_type=jnp.float32)
        return (new_q, (key_part, value_part))

    grad_q, (key_parts, value_parts) = lax.scan(
        backward_tile,
        jnp.zeros((row_total, width), jnp.float32),
        (key_tiles, value_tiles, tag_tiles, pos_tiles),
    )
    grads_win = jnp.concatenate(
        [
            key_parts.reshape(win_blocks * block_len, width),
            value_parts.reshape(win_blocks * block_len, width),
        ],
        axis=1,
    )
    canvas = jnp.zeros(((2 * span_blocks + pad_blocks) * block_len, 2 * width), jnp.float32)
    canvas = lax.dynamic_update_slice_in_dim(canvas, grads_win, first_block * block_len, 0)
    earlier_part = canvas[: span_blocks * block_len]
    group_part = canvas[span_blocks * block_len : 2 * span_blocks * block_len]
    combined = jnp.concatenate([group_part, earlier_part], axis=1)
    summed = lax.psum_scatter(
        combined.astype(jnp.bfloat16), "inner", scatter_dimension=0, tiled=True
    ).astype(jnp.float32)
    returned = shifted(summed[:, 2 * width :].astype(jnp.bfloat16), "outer", -1).astype(jnp.float32)
    grads_kv = summed[:, : 2 * width] + returned
    grad_queries = grad_q.reshape(token_count, head_count * width).astype(jnp.bfloat16)
    return (
        grad_queries,
        grads_kv[:, :width].astype(jnp.bfloat16),
        grads_kv[:, width:].astype(jnp.bfloat16),
    )


def solution(mesh):
    in_specs = (
        P(("outer", "inner"), None),
        P(("outer", "inner"), None),
        P(("outer", "inner"), None),
        P(("outer", "inner"), None),
        P(),
    )
    out_specs = (
        P(("outer", "inner"), None),
        P(("outer", "inner"), None),
        P(("outer", "inner"), None),
    )
    return jax.shard_map(shards, mesh=mesh, in_specs=in_specs, out_specs=out_specs, check_vma=False)
```

profile of v0, /device:TPU:6, one launch (start us, length us, event | category | flops | bytes accessed | tf_op | source)
XLA Modules:
  0.0 571.5 jit_solution(11450851049235379509)
XLA Ops:
  8.7 3.4 collective-permute-start
  12.1 2.6 collective-permute-done
  15.4 5.5 collective-permute-start.1
  20.9 1.9 collective-permute-done.1
  28.2 63.1 %all-gather.7.cloned.1.call-done = bf16[4096,128]{1,0:T(8,128)(2,1)} async-done(((bf16[128,128]{1,0:T(8,128)(2,1)}), bf16[4096,128]{1,0:T(8,128)(2,1)}) %all-gather.7.cloned.1.call-update) | async-done | bytes 1048592 | tf_op jit(solution)/shard_map/all_gather | solution.py:32
  91.2 77.2 %all-gather.11.cloned.1.call-done = bf16[4096,128]{1,0:T(8,128)(2,1)} async-done(((bf16[128,128]{1,0:T(8,128)(2,1)}), bf16[4096,128]{1,0:T(8,128)(2,1)}) %all-gather.11.cloned.1.call-update) | async-done | bytes 1048592 | tf_op jit(solution)/shard_map/all_gather | solution.py:33
  168.4 77.8 %all-gather.5.cloned.1.call-done = bf16[4096,128]{1,0:T(8,128)(2,1)} async-done(((bf16[128,128]{1,0:T(8,128)(2,1)}), bf16[4096,128]{1,0:T(8,128)(2,1)}) %all-gather.5.cloned.1.call-update) | async-done | bytes 1048592 | tf_op jit(solution)/shard_map/all_gather | solution.py:34
  246.2 77.6 %all-gather.9.cloned.1.call-done = bf16[4096,128]{1,0:T(8,128)(2,1)} async-done(((bf16[128,128]{1,0:T(8,128)(2,1)}), bf16[4096,128]{1,0:T(8,128)(2,1)}) %all-gather.9.cloned.1.call-update) | async-done | bytes 1048592 | tf_op jit(solution)/shard_map/all_gather | solution.py:35
  323.8 5.2 fusion.43
  329.1 35.2 %while.30 = (s32[]{:T(128)}, f32[1024,1]{0,1:T(1,128)S(1)}, f32[1024,1]{0,1:T(1,128)S(1)}, f32[1024,128]{1,0:T(8,128)S(1)}, s32[9,512]{1,0:T(8,128)S(1)}, /*inde...) while((s32[]{:T(128)}, f32[1024,1]{0,1:T(1,128)S(1)}, ...), condition=%wide.region_3.4_spmd.clone, body=%wide.region_0.3_spmd.clone.sunk | while | flops 410524160 | bytes 11240605 | solution.py:98
  329.9 1.6 fusion.84
  333.8 1.5 fusion.84
  337.7 1.5 fusion.84
  341.6 1.6 fusion.84
  349.5 1.5 fusion.84
  353.4 1.6 fusion.84
  357.3 1.5 fusion.84
  361.2 1.5 fusion.84
  364.7 60.3 %while.31 = (s32[]{:T(128)}, f32[1024,128]{1,0:T(8,128)S(1)}, bf16[9,512,128]{2,1,0:T(8,128)(2,1)}, bf16[9,512,128]{2,1,0:T(8,128)(2,1)}, s32[9,512]{1,0:T(8,128...) while((s32[]{:T(128)}, f32[1024,128]{1,0:T(8,128)S(1)}, ...), condition=%wide.region_6.7_spmd.clone, body=%wide.region_5.6_spmd.clone.sunk | while | flops 677119488 | bytes 12494019 | solution.py:122
  365.5 1.8 fusion.100
  372.2 1.7 fusion.100
  378.9 1.7 fusion.100
  385.6 1.7 fusion.100
  392.3 1.7 fusion.100
  399.0 1.8 fusion.100
  405.7 1.7 fusion.100
  412.4 1.8 fusion.100
  419.1 1.7 fusion.100
  427.4 2.3 pad_maximum_fusion
  429.7 124.6 %reduce-scatter.2.cloned.1.call-done = bf16[128,512]{1,0:T(8,128)(2,1)} async-done(((bf16[4096,512]{1,0:T(8,128)(2,1)}), bf16[128,512]{1,0:T(8,128)(2,1)}) %reduce-scatter.2.cloned.1.call-update) | async-done | bytes 131088 | tf_op jit(solution)/shard_map/reduce_scatter | solution.py:139
  555.2 2.9 collective-permute-start.2
  559.0 4.5 collective-permute-done.2
  (210 shorter events, 79.9 us)
Async XLA Ops:
  7.2 84.1 %all-gather.7.cloned.1.call-start = ((), (), s32[]{:S(2)}) async-start(), calls=%async_computation.2 | async-start | bytes 1081344 | tf_op jit(solution)/shard_map/all_gather | solution.py:32
  7.9 160.5 %all-gather.11.cloned.1.call-start = ((), (), s32[]{:S(2)}) async-start(), calls=%async_computation.4 | async-start | bytes 1081344 | tf_op jit(solution)/shard_map/all_gather | solution.py:33
  8.6 237.6 %all-gather.5.cloned.1.call-start = ((), (), s32[]{:S(2)}) async-start(), calls=%async_computation.1 | async-start | bytes 1081344 | tf_op jit(solution)/shard_map/all_gather | solution.py:34
  8.7 6.0 %collective-permute-start = (bf16[128,128]{1,0:T(8,128)(2,1)}, bf16[128,128]{1,0:T(8,128)(2,1)S(1)}, u32[]{:S(2)}, u32[]{:S(2)}) collective-permute-start(bf16[128,128]{1,0:T(8,128)(2,1)} %param.10), channel_id=1, source_target_pairs={{0,1},{1,2},{2,3},{3,4},{4,5},{5,6},{6,7},{8,9},{9,10},{10,11},{11... | collective-permute-start | bytes 98312 | tf_op jit(solution)/shard_map/ppermute | solution.py:10
  14.7 0.6 copy-start.2
  15.4 308.5 %all-gather.9.cloned.1.call-start = ((), (), s32[]{:S(2)}) async-start(), calls=%async_computation.3 | async-start | bytes 1081344 | tf_op jit(solution)/shard_map/all_gather | solution.py:35
  15.4 7.4 %collective-permute-start.1 = (bf16[128,128]{1,0:T(8,128)(2,1)}, bf16[128,128]{1,0:T(8,128)(2,1)S(1)}, u32[]{:S(2)}, u32[]{:S(2)}) collective-permute-start(bf16[128,128]{1,0:T(8,128)(2,1)} %param.11), channel_id=1, source_target_pairs={{0,1},{1,2},{2,3},{3,4},{4,5},{5,6},{6,7},{8,9},{9,10},{10,11},{11... | collective-permute-start | bytes 98312 | tf_op jit(solution)/shard_map/ppermute | solution.py:10
  22.8 0.6 copy-start.3
  23.4 530.9 %reduce-scatter.2.cloned.1.call-start = ((), (), s32[]{:S(2)}) async-start(), calls=%async_computation.5 | async-start | bytes 4325376 | tf_op jit(solution)/shard_map/reduce_scatter | solution.py:139
  425.0 1.3 copy-start
  425.0 1.6 copy-start.1
  555.2 8.3 %collective-permute-start.2 = (bf16[128,256]{1,0:T(8,128)(2,1)S(1)}, bf16[128,256]{1,0:T(8,128)(2,1)S(1)}, u32[]{:S(2)}, u32[]{:S(2)}) collective-permute-start(bf16[128,256]{1,0:T(8,128)(2,1)S(1)} %slice.36), channel_id=1, source_target_pairs={{1,0},{2,1},{3,2},{4,3},{5,4},{6,5},{7,6},{9,8},{10,9},{11,10},{12... | collective-permute-start | bytes 196616 | tf_op jit(solution)/shard_map/ppermute | solution.py:10
Sparse Core Ops, SparseCore 0:
  10.8 80.4 all-gather.6
  94.0 74.3 all-gather.10
  171.8 74.3 all-gather.4
  249.4 74.3 all-gather.8
  429.8 124.4 reduce-scatter.1
where the time goes:
time: 573 us; the launch traced here: 571 us
  waiting for transfers between devices  431 us (75%)
  matrix products  77.1 us (13%)
  other arithmetic  25.6 us (4%)
  between operations  13.9 us (2%)
  starting transfers between devices  12 us (2%)
  local copies, waits for them, and re-layouts  11 us (2%)
    reduce_scatter x1, waiting for transfers between devices, shards(): lax.psum_scatter(combined.astype(jnp.bfloat16), 'inner', scatter_dimensio...  125 us
    all_gather x1, waiting for transfers between devices, shards(): lax.all_gather(earlier_k, 'inner', axis=0, tiled=True)  77.8 us
    all_gather x1, waiting for transfers between devices, shards(): lax.all_gather(earlier_v, 'inner', axis=0, tiled=True)  77.6 us
    all_gather x1, waiting for transfers between devices, shards(): lax.all_gather(value_rows, 'inner', axis=0, tiled=True)  77.2 us
    all_gather x1, waiting for transfers between devices, shards(): lax.all_gather(key_rows, 'inner', axis=0, tiled=True)  63.1 us
    dot_general x9, matrix products, backward_tile(): jnp.einsum('rd,kd->rk', query_flat, key_tile, preferred_element_type=jnp....  15.7 us
    dot_general x9, matrix products, forward_tile(): jnp.einsum('rd,kd->rk', query_flat, key_tile, preferred_element_type=jnp....  13.9 us
    dot_general x9, matrix products, backward_tile(): jnp.dot(dscores, key_tile, preferred_element_type=jnp.float32)  13.5 us
  transfers between devices with their start and end apart: 8, of which 8 were waited for; matrix products, arithmetic and copies ran while one was open for 1% of the time, Pallas kernels for 0%

commit v1 on v0

--- a/solution.py
+++ b/solution.py
@@ -32,7 +32,9 @@
         lax.all_gather(key_rows, "inner", axis=0, tiled=True),
         lax.all_gather(value_rows, "inner", axis=0, tiled=True),
         lax.all_gather(earlier_k, "inner", axis=0, tiled=True),
-        lax.all_gather(earlier_v, "inner", axis=0, tiled=True),
+        jnp.concatenate(
+            lax.all_to_all(jnp.stack([earlier_v] * lax.axis_size("inner")), "inner", 0, 0), axis=0
+        ),
     )
     padding = jnp.zeros((pad_blocks * block_len, width), key_rows.dtype)
     keys_all = jnp.concatenate([prior_k, group_k, padding], axis=0)

time: 573 us -> 498 us (0.87)
  waiting for transfers between devices: 431 us -> 351 us
  starting transfers between devices: 12 us -> 20.9 us
    all_gather x1 -> x0, waiting for transfers between devices: 77.6 us -> none  [shards(): lax.all_gather(earlier_v, 'inner', axis=0, tiled=True)]
    all_to_all x0 -> x1, starting transfers between devices: none -> 11.2 us  [shards(): lax.all_to_all(jnp.stack([earlier_v] * lax.axis_size('inner')), 'inner',...]
  transfers between devices with their start and end apart: 8 -> 8, of which waited for: 8 -> 6; matrix products, arithmetic and copies ran while one was open for 1% -> 1% of each run, Pallas kernels for 0% -> 0%
where the time goes in v1:
time: 498 us; the launch traced here: 497 us
  waiting for transfers between devices  351 us (70%)
  matrix products  77 us (15%)
  other arithmetic  23.2 us (5%)
  starting transfers between devices  20.9 us (4%)
  between operations  14 us (3%)
  local copies, waits for them, and re-layouts  10 us (2%)
    reduce_scatter x1, waiting for transfers between devices, shards(): lax.psum_scatter(combined.astype(jnp.bfloat16), 'inner', scatter_dimensio...  125 us
    all_gather x1, waiting for transfers between devices, shards(): lax.all_gather(earlier_k, 'inner', axis=0, tiled=True)  77.8 us
    all_gather x1, waiting for transfers between devices, shards(): lax.all_gather(value_rows, 'inner', axis=0, tiled=True)  77.2 us
    all_gather x1, waiting for transfers between devices, shards(): lax.all_gather(key_rows, 'inner', axis=0, tiled=True)  63.1 us
    dot_general x9, matrix products, backward_tile(): jnp.einsum('rd,kd->rk', query_flat, key_tile, preferred_element_type=jnp....  15.7 us
    dot_general x9, matrix products, forward_tile(): jnp.einsum('rd,kd->rk', query_flat, key_tile, preferred_element_type=jnp....  13.9 us
    dot_general x9, matrix products, backward_tile(): jnp.dot(dscores, key_tile, preferred_element_type=jnp.float32)  13.5 us
    all_to_all x1, starting transfers between devices, shards(): lax.all_to_all(jnp.stack([earlier_v] * lax.axis_size('inner')), 'inner',...  11.2 us
  transfers between devices with their start and end apart: 8, of which 6 were waited for; matrix products, arithmetic and copies ran while one was open for 1% of the time, Pallas kernels for 0%

profile of v1, /device:TPU:6, one launch (start us, length us, event | category | flops | bytes accessed | tf_op | source)
XLA Modules:
  0.0 497.1 jit_solution(15244704757231253730)
XLA Ops:
  8.7 3.4 collective-permute-start
  12.1 3.4 collective-permute-start.1
  16.2 2.0 collective-permute-done.1
  19.4 11.2 %all-to-all-start = ((bf16[32,128,128]{2,1,0:T(8,128)(2,1)}), bf16[32,128,128]{2,1,0:T(8,128)(2,1)S(1)}, u32[]{:S(2)}, u32[]{:S(2)}) async-start(bf16[32,128,128]{2,1,0:T(8,128)(2,1)} %stack.2), calls=%async_computation | async-start | bytes 2097152 | tf_op jit(solution)/shard_map/all_to_all | solution.py:36
  32.0 63.1 %all-gather.6.cloned.1.call-done = bf16[4096,128]{1,0:T(8,128)(2,1)} async-done(((bf16[128,128]{1,0:T(8,128)(2,1)}), bf16[4096,128]{1,0:T(8,128)(2,1)}) %all-gather.6.cloned.1.call-update) | async-done | bytes 1048592 | tf_op jit(solution)/shard_map/all_gather | solution.py:32
  95.1 77.2 %all-gather.8.cloned.1.call-done = bf16[4096,128]{1,0:T(8,128)(2,1)} async-done(((bf16[128,128]{1,0:T(8,128)(2,1)}), bf16[4096,128]{1,0:T(8,128)(2,1)}) %all-gather.8.cloned.1.call-update) | async-done | bytes 1048592 | tf_op jit(solution)/shard_map/all_gather | solution.py:33
  172.3 77.8 %all-gather.4.cloned.1.call-done = bf16[4096,128]{1,0:T(8,128)(2,1)} async-done(((bf16[128,128]{1,0:T(8,128)(2,1)}), bf16[4096,128]{1,0:T(8,128)(2,1)}) %all-gather.4.cloned.1.call-update) | async-done | bytes 1048592 | tf_op jit(solution)/shard_map/all_gather | solution.py:34
  251.1 5.2 %fusion.43 = (bf16[4608,128]{1,0:T(8,128)(2,1)S(1)}, bf16[4608,128]{1,0:T(8,128)(2,1)}) fusion(s32[]{:T(128)S(6)} %select_n.20, bf16[4096,128]{1,0:T(8,128)(2,1)} %bitcast.126, bf16[4096,128]{1,0:T(8,128)(2,1)} %all-gather.8.cloned.1.call-done, bf16[4608]{0:T(1024)(128)(2,1)S(1)} %pad_dynamic-slice_fusion.4, ...), kind=kLoop, calls=%fused_computation.65 | loop fusion | flops 6488064 | bytes 6562820 | tf_op jit(solution)/shard_map/concatenate | solution.py:41
  256.3 34.3 %while.30 = (s32[]{:T(128)}, f32[1024,1]{0,1:T(1,128)S(1)}, f32[1024,1]{0,1:T(1,128)S(1)}, f32[1024,128]{1,0:T(8,128)S(1)}, s32[9,512]{1,0:T(8,128)S(1)}, /*inde...) while((s32[]{:T(128)}, f32[1024,1]{0,1:T(1,128)S(1)}, ...), condition=%wide.region_3.4_spmd.clone, body=%wide.region_0.3_spmd.clone.sunk | while | flops 410524160 | bytes 11240605 | solution.py:100
  257.0 1.6 fusion.84
  260.8 1.5 fusion.84
  264.6 1.5 fusion.84
  268.5 1.5 fusion.84
  272.3 1.5 fusion.84
  276.1 1.5 fusion.84
  279.9 1.5 fusion.84
  283.7 1.5 fusion.84
  287.5 1.5 fusion.84
  291.0 59.4 %while.31 = (s32[]{:T(128)}, f32[1024,128]{1,0:T(8,128)S(1)}, bf16[9,512,128]{2,1,0:T(8,128)(2,1)}, bf16[9,512,128]{2,1,0:T(8,128)(2,1)}, s32[9,512]{1,0:T(8,128...) while((s32[]{:T(128)}, f32[1024,128]{1,0:T(8,128)S(1)}, ...), condition=%wide.region_6.7_spmd.clone, body=%wide.region_5.6_spmd.clone.sunk | while | flops 677119488 | bytes 12494019 | solution.py:124
  291.7 1.7 fusion.100
  298.3 1.7 fusion.100
  304.9 1.8 fusion.100
  311.5 1.7 fusion.100
  318.1 1.7 fusion.100
  324.7 1.7 fusion.100
  331.3 1.7 fusion.100
  337.9 1.7 fusion.100
  344.5 1.7 fusion.100
  352.8 2.3 pad_maximum_fusion
  355.1 124.9 %reduce-scatter.2.cloned.1.call-done = bf16[128,512]{1,0:T(8,128)(2,1)} async-done(((bf16[4096,512]{1,0:T(8,128)(2,1)}), bf16[128,512]{1,0:T(8,128)(2,1)}) %reduce-scatter.2.cloned.1.call-update) | async-done | bytes 131088 | tf_op jit(solution)/shard_map/reduce_scatter | solution.py:141
  480.8 2.8 collective-permute-start.2
  484.5 4.6 collective-permute-done.2
  (216 shorter events, 74.8 us)
Async XLA Ops:
  7.2 23.5 %copy-start.6 = (s32[256]{0:T(256)S(1)}, s32[256]{0:T(256)}, u32[]{:S(2)}) copy-start(s32[256]{0:T(256)} %param.13) | copy-start | bytes 3076
  7.2 24.5 %copy-start.3 = (bf16[128,1024]{1,0:T(8,128)(2,1)S(1)}, bf16[128,1024]{1,0:T(8,128)(2,1)}, u32[]{:S(2)}) copy-start(bf16[128,1024]{1,0:T(8,128)(2,1)} %param.9) | copy-start | bytes 786436
  7.2 24.6 %copy-start.4 = (bf16[128,1024]{1,0:T(8,128)(2,1)S(1)}, bf16[128,1024]{1,0:T(8,128)(2,1)}, u32[]{:S(2)}) copy-start(bf16[128,1024]{1,0:T(8,128)(2,1)} %param.12) | copy-start | bytes 786436
  7.2 87.9 %all-gather.6.cloned.1.call-start = ((), (), s32[]{:S(2)}) async-start(), calls=%async_computation.3 | async-start | bytes 1081344 | tf_op jit(solution)/shard_map/all_gather | solution.py:32
  7.9 164.4 %all-gather.8.cloned.1.call-start = ((), (), s32[]{:S(2)}) async-start(), calls=%async_computation.4 | async-start | bytes 1081344 | tf_op jit(solution)/shard_map/all_gather | solution.py:33
  8.7 241.4 %all-gather.4.cloned.1.call-start = ((), (), s32[]{:S(2)}) async-start(), calls=%async_computation.2 | async-start | bytes 1081344 | tf_op jit(solution)/shard_map/all_gather | solution.py:34
  8.7 6.8 %collective-permute-start = (bf16[128,128]{1,0:T(8,128)(2,1)}, bf16[128,128]{1,0:T(8,128)(2,1)S(1)}, u32[]{:S(2)}, u32[]{:S(2)}) collective-permute-start(bf16[128,128]{1,0:T(8,128)(2,1)} %param.10), channel_id=1, source_target_pairs={{0,1},{1,2},{2,3},{3,4},{4,5},{5,6},{6,7},{8,9},{9,10},{10,11},{11... | collective-permute-start | bytes 98312 | tf_op jit(solution)/shard_map/ppermute | solution.py:10
  12.1 6.0 %collective-permute-start.1 = (bf16[128,128]{1,0:T(8,128)(2,1)}, bf16[128,128]{1,0:T(8,128)(2,1)S(1)}, u32[]{:S(2)}, u32[]{:S(2)}) collective-permute-start(bf16[128,128]{1,0:T(8,128)(2,1)} %param.11), channel_id=1, source_target_pairs={{0,1},{1,2},{2,3},{3,4},{4,5},{5,6},{6,7},{8,9},{9,10},{10,11},{11... | collective-permute-start | bytes 98312 | tf_op jit(solution)/shard_map/ppermute | solution.py:10
  15.5 0.6 copy-start.5
  19.4 230.7 %all-to-all-start = ((bf16[32,128,128]{2,1,0:T(8,128)(2,1)}), bf16[32,128,128]{2,1,0:T(8,128)(2,1)S(1)}, u32[]{:S(2)}, u32[]{:S(2)}) async-start(bf16[32,128,128]{2,1,0:T(8,128)(2,1)} %stack.2), calls=%async_computation | async-start | bytes 2097152 | tf_op jit(solution)/shard_map/all_to_all | solution.py:36
  30.6 449.4 %reduce-scatter.2.cloned.1.call-start = ((), (), s32[]{:S(2)}) async-start(), calls=%async_computation.5 | async-start | bytes 4325376 | tf_op jit(solution)/shard_map/reduce_scatter | solution.py:141
  250.1 1.0 copy-start
  350.4 1.3 copy-start.1
  350.4 1.6 copy-start.2
  480.8 8.3 %collective-permute-start.2 = (bf16[128,256]{1,0:T(8,128)(2,1)S(1)}, bf16[128,256]{1,0:T(8,128)(2,1)S(1)}, u32[]{:S(2)}, u32[]{:S(2)}) collective-permute-start(bf16[128,256]{1,0:T(8,128)(2,1)S(1)} %slice.36), channel_id=1, source_target_pairs={{1,0},{2,1},{3,2},{4,3},{5,4},{6,5},{7,6},{9,8},{10,9},{11,10},{12... | collective-permute-start | bytes 196616 | tf_op jit(solution)/shard_map/ppermute | solution.py:10
Sparse Core Ops, SparseCore 0:
  10.8 84.2 all-gather.5
  97.9 74.3 all-gather.7
  175.7 74.3 all-gather.3
  355.2 124.7 reduce-scatter.1
